TPU v7x, 512 devices: a whole 4x4x16 slice. The times are simulated.
512 devices in a mesh: ctx: 64 (over z, y), tp: 8 (over x, core).
Axes of the slice: x: 4, y: 4, z: 16, core: 2. Of those that a mesh axis runs over, the one named last changes fastest.
Arguments:
- queries: bfloat16 [8192, 4096], P('ctx', 'tp'), may hold values from -6 to 6
- keys: bfloat16 [8192, 1024], P('ctx', 'tp'), may hold values from -6 to 6
- values: bfloat16 [8192, 1024], P('ctx', 'tp'), may hold values from -4 to 4
- w_out: bfloat16 [4096, 4096], P('tp'), may hold values from -0.09375 to 0.09375
- relevance_out: bfloat16 [8192, 4096], P('ctx', 'tp'), may hold values from -4 to 4
- segment_ids: int32 [8192], replicated, may hold values from 0 to 31, never falling along the last dimension, each value on 1 to 1024 neighbouring positions
Outputs:
- relevance_heads: bfloat16 [8192, 4096], P('ctx', 'tp')
- relevance_tokens: float32 [8192, 8], P('ctx', 'tp')
Inputs may be any that keep to these rules, and one draw needn't show every extreme that they name: `segment_ids`: ids never fall along the prompt; every document holds 1 to 1024 tokens and one holds exactly 1024.
All inputs are finite; a program needn't handle non-finite values.
Results may differ from a plain program's by a relative error of at most 0.02.
Values may be sent and summed in bfloat16 or wider, within the bound.
A program may use at most 64 MiB of HBM per device.

v0:
```python
import jax
import jax.numpy as jnp
from jax import lax
from jax.sharding import PartitionSpec as P

HEAD_DIM = 128
REACH = 8
KBLK = 512
GROUP = 4
masked_score = -1e30


def passed_along(shard, axis, by):
    count = lax.axis_size(axis)
    pairs = [(i, i + by) for i in range(count) if 0 <= i + by < count]
    return lax.ppermute(shard, axis, pairs)


def masked_scores(query_rows, key_block, row_segment, row_position, key_segment, key_position):
    scores = jnp.einsum(
        "krd,jkd->krj", query_rows, key_block, preferred_element_type=jnp.float32
    ) * HEAD_DIM ** (-0.5)
    visible = (row_segment[:, None] == key_segment[None, :]) & (
        key_position[None, :] <= row_position[:, None]
    )
    return (scores, visible[None])


def to_rows(matrix, tokens, local_groups):
    return (
        matrix.reshape(tokens, local_groups, GROUP, HEAD_DIM)
        .transpose(1, 0, 2, 3)
        .reshape(local_groups, tokens * GROUP, HEAD_DIM)
    )


def on_device(queries, keys, values, w_out, relevance_out, segment_ids):
    tokens = queries.shape[0]
    local_groups = keys.shape[1] // HEAD_DIM
    row_count = tokens * GROUP
    shard_index = lax.axis_index("ctx")
    first_token = shard_index * tokens
    query_rows = to_rows(queries, tokens, local_groups)
    own_segment = lax.dynamic_slice_in_dim(segment_ids, first_token, tokens)
    row_segment = jnp.repeat(own_segment, GROUP)
    row_position = first_token + jnp.repeat(jnp.arange(tokens, dtype=jnp.int32), GROUP)
    earlier = []
    for distance in range(REACH, 0, -1):
        earlier.append(passed_along((keys, values), "ctx", distance))
    window_length = ((REACH + 1) * tokens + KBLK - 1) // KBLK * KBLK
    pad_rows = window_length - (REACH + 1) * tokens
    filler = jnp.zeros((pad_rows, keys.shape[1]), keys.dtype)
    key_window = jnp.concatenate([piece[0] for piece in earlier] + [keys, filler], axis=0)
    value_window = jnp.concatenate([piece[1] for piece in earlier] + [values, filler], axis=0)
    offset = first_token - REACH * tokens
    padded_segments = jnp.concatenate(
        [
            jnp.full((window_length,), -1, jnp.int32),
            segment_ids,
            jnp.full((window_length,), -1, jnp.int32),
        ]
    )
    key_segment = lax.dynamic_slice_in_dim(padded_segments, offset + window_length, window_length)
    key_heads = key_window.reshape(window_length, local_groups, HEAD_DIM)
    value_heads = value_window.reshape(window_length, local_groups, HEAD_DIM)
    doc_start = jnp.sum((segment_ids < own_segment[0]).astype(jnp.int32))
    low_block = (doc_start - offset) // KBLK
    high_block = (first_token + tokens - 1 - offset) // KBLK + 1

    def block_inputs(block):
        start = block * KBLK
        key_block = lax.dynamic_slice_in_dim(key_heads, start, KBLK, 0)
        value_block = lax.dynamic_slice_in_dim(value_heads, start, KBLK, 0)
        segment_block = lax.dynamic_slice_in_dim(key_segment, start, KBLK)
        position_block = offset + start + jnp.arange(KBLK, dtype=jnp.int32)
        scores, visible = masked_scores(
            query_rows, key_block, row_segment, row_position, segment_block, position_block
        )
        return (start, value_block, scores, visible)

    def forward_block(block, carry):
        row_max, total, summed = carry
        start, value_block, scores, visible = block_inputs(block)
        new_max = jnp.maximum(row_max, jnp.max(jnp.where(visible, scores, masked_score), axis=2))
        weights = jnp.where(visible, jnp.exp(scores - new_max[..., None]), 0.0)
        rescale = jnp.exp(row_max - new_max)
        total = total * rescale + jnp.sum(weights, axis=2)
        summed = summed * rescale[..., None] + jnp.einsum(
            "krj,jkd->krd",
            weights.astype(jnp.bfloat16),
            value_block,
            preferred_element_type=jnp.float32,
        )
        return (new_max, total, summed)

    start_carry = (
        jnp.full((local_groups, row_count), masked_score, jnp.float32),
        jnp.zeros((local_groups, row_count), jnp.float32),
        jnp.zeros((local_groups, row_count, HEAD_DIM), jnp.float32),
    )
    row_max, total, summed = lax.fori_loop(low_block, high_block, forward_block, start_carry)
    attention_rows = (summed / total[..., None]).astype(jnp.bfloat16)
    attention = (
        attention_rows.reshape(local_groups, tokens, GROUP, HEAD_DIM)
        .transpose(1, 0, 2, 3)
        .reshape(tokens, local_groups * GROUP * HEAD_DIM)
    )
    totals = lax.psum(jnp.dot(attention, w_out, preferred_element_type=jnp.float32), "tp")
    upper = lax.all_gather(relevance_out, "tp", axis=1, tiled=True).astype(jnp.float32)
    ratio = (upper * totals / (totals * totals + 1.0)).astype(jnp.bfloat16)
    carried_back = lax.dot_general(
        ratio, w_out, (((1,), (1,)), ((), ())), preferred_element_type=jnp.float32
    )
    attention_float = attention.astype(jnp.float32)
    carried = attention_float * carried_back
    relevance_heads = carried.astype(jnp.bfloat16)
    passed = (carried * attention_float / (attention_float * attention_float + 1.0)).astype(
        jnp.bfloat16
    )
    passed_rows = to_rows(passed, tokens, local_groups)

    def backward_block(block, terms):
        start, value_block, scores, visible = block_inputs(block)
        share = jnp.where(visible, jnp.exp(scores - row_max[..., None]), 0.0) / total[..., None]
        inner = jnp.einsum(
            "krd,jkd->krj", passed_rows, value_block, preferred_element_type=jnp.float32
        )
        added = jnp.sum(share * inner, axis=1)
        current = lax.dynamic_slice_in_dim(terms, start, KBLK, 1)
        return lax.dynamic_update_slice_in_dim(terms, current + added, start, 1)

    terms = lax.fori_loop(
        low_block, high_block, backward_block, jnp.zeros((local_groups, window_length), jnp.float32)
    )
    own_terms = lax.dynamic_slice_in_dim(terms, first_token - offset, tokens, 1)
    for distance in range(1, REACH + 1):
        piece = lax.dynamic_slice_in_dim(terms, first_token - distance * tokens - offset, tokens, 1)
        own_terms = own_terms + passed_along(piece, "ctx", -distance)
    return (relevance_heads, own_terms.T)


def solution(mesh):
    placed = (P("ctx", "tp"), P("ctx", "tp"), P("ctx", "tp"), P("tp", None), P("ctx", "tp"), P())
    return jax.shard_map(
        on_device,
        mesh=mesh,
        in_specs=placed,
        out_specs=(P("ctx", "tp"), P("ctx", "tp")),
        check_vma=False,
    )
```

profile of v0, /device:TPU:448, one launch (start us, length us, event | category | flops | bytes accessed | tf_op | source)
XLA Modules:
  0.0 242.1 jit_solution(6290647112543033285)
XLA Ops:
  8.5 5.4 %collective-permute-start.1 = (bf16[128,128]{1,0:T(8,128)(2,1)}, bf16[128,128]{1,0:T(8,128)(2,1)S(1)}, u32[]{:S(2)}, u32[]{:S(2)}) collective-permute-start(bf16[128,128]{1,0:T(8,128)(2,1)} %param.11), channel_id=1, source_target_pairs={{0,56},{8,64},{16,72},{24,80},{32,88},{40,96},{48,104},{56,112},{6... | collective-permute-start | bytes 98312 | tf_op jit(solution)/shard_map/ppermute | solution.py:16
  13.9 1.9 collective-permute-start.2
  26.3 2.1 collective-permute-start.6
  28.5 1.9 collective-permute-start.7
  31.8 1.9 collective-permute-start.9
  33.7 1.9 collective-permute-start.10
  35.7 1.9 collective-permute-start.11
  41.0 3.3 %collective-permute-start.13 = (bf16[128,128]{1,0:T(8,128)(2,1)}, bf16[128,128]{1,0:T(8,128)(2,1)S(1)}, u32[]{:S(2)}, u32[]{:S(2)}) collective-permute-start(bf16[128,128]{1,0:T(8,128)(2,1)} %param.12), channel_id=1, source_target_pairs={{0,24},{8,32},{16,40},{24,48},{32,56},{40,64},{48,72},{56,80},{64,... | collective-permute-start | bytes 98312 | tf_op jit(solution)/shard_map/ppermute | solution.py:16
  44.4 2.9 %collective-permute-start.14 = (bf16[128,128]{1,0:T(8,128)(2,1)}, bf16[128,128]{1,0:T(8,128)(2,1)S(1)}, u32[]{:S(2)}, u32[]{:S(2)}) collective-permute-start(bf16[128,128]{1,0:T(8,128)(2,1)} %param.12), channel_id=1, source_target_pairs={{0,16},{8,24},{16,32},{24,40},{32,48},{40,56},{48,64},{56,72},{64,... | collective-permute-start | bytes 98312 | tf_op jit(solution)/shard_map/ppermute | solution.py:16
  49.6 3.4 %collective-permute-done.14 = bf16[128,128]{1,0:T(8,128)(2,1)S(1)} collective-permute-done((bf16[128,128]{1,0:T(8,128)(2,1)}, bf16[128,128]{1,0:T(8,128)(2,1)S(1)}, u32[]{:S(2)}, u32[]{:S(2)}) %collective-permute-start.14) | collective-permute-done | bytes 32800 | tf_op jit(solution)/shard_map/ppermute | solution.py:16
  53.0 2.4 %collective-permute-done.15 = bf16[128,128]{1,0:T(8,128)(2,1)S(1)} collective-permute-done((bf16[128,128]{1,0:T(8,128)(2,1)}, bf16[128,128]{1,0:T(8,128)(2,1)S(1)}, u32[]{:S(2)}, u32[]{:S(2)}) %collective-permute-start.15) | collective-permute-done | bytes 32800 | tf_op jit(solution)/shard_map/ppermute | solution.py:16
  56.3 3.6 %while.26 = (s32[]{:T(128)}, f32[1,512]{1,0:T(1,128)S(1)}, f32[1,512]{1,0:T(1,128)S(1)}, f32[1,512,128]{2,1,0:T(8,128)S(1)}, s32[]{:T(128)}, /*index=5*/s32[1536...) while((s32[]{:T(128)}, f32[1,512]{1,0:T(1,128)S(1)}, ...), condition=%wide.region_4.5_spmd.clone, body=%wide.region_1.4_spmd.clone.sunk | while | flops 139069440 | bytes 4139747 | solution.py:101
  60.2 4.3 %fusion.48 = f32[128,4096]{1,0:T(8,128)} fusion(bf16[128,512]{1,0:T(8,128)(2,1)S(1)} %reshape_transpose_reshape.10, bf16[512,4096]{1,0:T(8,128)(2,1)} %param.13), kind=kOutput, calls=%fused_computation.94 | convolution fusion | flops 536870912 | bytes 6422528 | tf_op jit(solution)/shard_map/dot_general | solution.py:108
  65.2 93.4 %all-reduce.2.cloned.1.call-done = f32[128,4096]{1,0:T(8,128)} async-done(((f32[128,4096]{1,0:T(8,128)}), f32[128,4096]{1,0:T(8,128)}) %all-reduce.2.cloned.1.call-update) | async-done | bytes 2097168 | tf_op jit(solution)/shard_map/psum | solution.py:108
  158.6 32.8 %all-gather.2.cloned.1.call-done = bf16[128,4096]{1,0:T(8,128)(2,1)} async-done(((bf16[128,512]{1,0:T(8,128)(2,1)}), bf16[128,4096]{1,0:T(8,128)(2,1)}) %all-gather.2.cloned.1.call-update) | async-done | bytes 1048592 | tf_op jit(solution)/shard_map/all_gather | solution.py:109
  191.4 5.3 %fusion.43 = (bf16[128,512]{1,0:T(8,128)(2,1)S(1)}, bf16[128,512]{1,0:T(8,128)(2,1)}) fusion(bf16[128,512]{1,0:T(8,128)(2,1)S(1)} %reshape_transpose_reshape.10, bf16[512,4096]{1,0:T(8,128)(2,1)} %param.13, f32[128,4096]{1,0:T(8,128)} %all-reduce.2.cloned.1.call-done, bf16[128,4096]{1,0:T(8,128)(2,1)} %all-gather.2.cloned.1.call-done), kind=kOutput, calls=%fused_computation.56 | convolution fusion | flops 540540928 | bytes 7733248 | tf_op jit(solution)/shard_map/dot_general | solution.py:111
  196.8 2.5 %while.27 = (s32[]{:T(128)}, f32[1,1536]{1,0:T(1,128)S(1)}, s32[]{:T(128)}, s32[1536]{0:T(1024)S(1)}, s32[]{:T(128)}, /*index=5*/bf16[1536,1,128]{2,0,1:T(8,128)...) while((s32[]{:T(128)}, f32[1,1536]{1,0:T(1,128)S(1)}, ...), condition=%wide.region_8.9_spmd.clone, body=%wide.region_6.8_spmd.clone.sunk | while | flops 136578048 | bytes 2661103 | solution.py:132
  199.4 5.5 %collective-permute-start.16 = (f32[1,128]{1,0:T(1,128)S(1)}, f32[1,128]{1,0:T(1,128)S(1)}, u32[]{:S(2)}, u32[]{:S(2)}) collective-permute-start(f32[1,128]{1,0:T(1,128)S(1)} %get-tuple-element.257), channel_id=1, source_target_pairs={{8,0},{16,8},{24,16},{32,24},{40,32},{48,40},{56,48},{64,56},{72,6... | collective-permute-start | bytes 1544 | tf_op jit(solution)/shard_map/ppermute | solution.py:16
  204.9 2.7 %collective-permute-start.17 = (f32[1,128]{1,0:T(1,128)S(1)}, f32[1,128]{1,0:T(1,128)S(1)}, u32[]{:S(2)}, u32[]{:S(2)}) collective-permute-start(f32[1,128]{1,0:T(1,128)S(1)} %get-tuple-element.263), channel_id=1, source_target_pairs={{16,0},{24,8},{32,16},{40,24},{48,32},{56,40},{64,48},{72,56},{80,... | collective-permute-start | bytes 1544 | tf_op jit(solution)/shard_map/ppermute | solution.py:16
  207.6 3.6 %collective-permute-start.18 = (f32[1,128]{1,0:T(1,128)S(1)}, f32[1,128]{1,0:T(1,128)S(1)}, u32[]{:S(2)}, u32[]{:S(2)}) collective-permute-start(f32[1,128]{1,0:T(1,128)S(1)} %get-tuple-element.262), channel_id=1, source_target_pairs={{24,0},{32,8},{40,16},{48,24},{56,32},{64,40},{72,48},{80,56},{88,... | collective-permute-start | bytes 1544 | tf_op jit(solution)/shard_map/ppermute | solution.py:16
  211.2 4.5 %collective-permute-start.19 = (f32[1,128]{1,0:T(1,128)S(1)}, f32[1,128]{1,0:T(1,128)S(1)}, u32[]{:S(2)}, u32[]{:S(2)}) collective-permute-start(f32[1,128]{1,0:T(1,128)S(1)} %get-tuple-element.261), channel_id=1, source_target_pairs={{32,0},{40,8},{48,16},{56,24},{64,32},{72,40},{80,48},{88,56},{96,... | collective-permute-start | bytes 1544 | tf_op jit(solution)/shard_map/ppermute | solution.py:16
  215.7 6.3 %collective-permute-start.20 = (f32[1,128]{1,0:T(1,128)S(1)}, f32[1,128]{1,0:T(1,128)S(1)}, u32[]{:S(2)}, u32[]{:S(2)}) collective-permute-start(f32[1,128]{1,0:T(1,128)S(1)} %get-tuple-element.260), channel_id=1, source_target_pairs={{40,0},{48,8},{56,16},{64,24},{72,32},{80,40},{88,48},{96,56},{104... | collective-permute-start | bytes 1544 | tf_op jit(solution)/shard_map/ppermute | solution.py:16
  222.1 5.0 %collective-permute-start.21 = (f32[1,128]{1,0:T(1,128)S(1)}, f32[1,128]{1,0:T(1,128)S(1)}, u32[]{:S(2)}, u32[]{:S(2)}) collective-permute-start(f32[1,128]{1,0:T(1,128)S(1)} %get-tuple-element.259), channel_id=1, source_target_pairs={{48,0},{56,8},{64,16},{72,24},{80,32},{88,40},{96,48},{104,56},{11... | collective-permute-start | bytes 1544 | tf_op jit(solution)/shard_map/ppermute | solution.py:16
  230.7 4.0 %collective-permute-done.22 = f32[1,128]{1,0:T(1,128)S(1)} collective-permute-done((f32[1,128]{1,0:T(1,128)S(1)}, f32[1,128]{1,0:T(1,128)S(1)}, u32[]{:S(2)}, u32[]{:S(2)}) %collective-permute-start.22) | collective-permute-done | bytes 544 | tf_op jit(solution)/shard_map/ppermute | solution.py:16
  (110 shorter events, 30.0 us)
Async XLA Ops:
  7.2 151.4 %all-reduce.2.cloned.1.call-start = ((), (), s32[]{:S(2)}) async-start(), calls=%async_computation.1 | async-start | bytes 4194304 | tf_op jit(solution)/shard_map/psum | solution.py:108
  7.2 17.2 %collective-permute-start = (bf16[128,128]{1,0:T(8,128)(2,1)}, bf16[128,128]{1,0:T(8,128)(2,1)S(1)}, u32[]{:S(2)}, u32[]{:S(2)}) collective-permute-start(bf16[128,128]{1,0:T(8,128)(2,1)} %param.11), channel_id=1, source_target_pairs={{0,64},{8,72},{16,80},{24,88},{32,96},{40,104},{48,112},{56,120},{... | collective-permute-start | bytes 98312 | tf_op jit(solution)/shard_map/ppermute | solution.py:16
  8.5 17.8 %collective-permute-start.1 = (bf16[128,128]{1,0:T(8,128)(2,1)}, bf16[128,128]{1,0:T(8,128)(2,1)S(1)}, u32[]{:S(2)}, u32[]{:S(2)}) collective-permute-start(bf16[128,128]{1,0:T(8,128)(2,1)} %param.11), channel_id=1, source_target_pairs={{0,56},{8,64},{16,72},{24,80},{32,88},{40,96},{48,104},{56,112},{6... | collective-permute-start | bytes 98312 | tf_op jit(solution)/shard_map/ppermute | solution.py:16
  13.9 14.6 %collective-permute-start.2 = (bf16[128,128]{1,0:T(8,128)(2,1)}, bf16[128,128]{1,0:T(8,128)(2,1)S(1)}, u32[]{:S(2)}, u32[]{:S(2)}) collective-permute-start(bf16[128,128]{1,0:T(8,128)(2,1)} %param.11), channel_id=1, source_target_pairs={{0,48},{8,56},{16,64},{24,72},{32,80},{40,88},{48,96},{56,104},{64... | collective-permute-start | bytes 98312 | tf_op jit(solution)/shard_map/ppermute | solution.py:16
  15.8 14.6 %collective-permute-start.3 = (bf16[128,128]{1,0:T(8,128)(2,1)}, bf16[128,128]{1,0:T(8,128)(2,1)S(1)}, u32[]{:S(2)}, u32[]{:S(2)}) collective-permute-start(bf16[128,128]{1,0:T(8,128)(2,1)} %param.11), channel_id=1, source_target_pairs={{0,40},{8,48},{16,56},{24,64},{32,72},{40,80},{48,88},{56,96},{64,... | collective-permute-start | bytes 98312 | tf_op jit(solution)/shard_map/ppermute | solution.py:16
  17.8 14.0 %collective-permute-start.4 = (bf16[128,128]{1,0:T(8,128)(2,1)}, bf16[128,128]{1,0:T(8,128)(2,1)S(1)}, u32[]{:S(2)}, u32[]{:S(2)}) collective-permute-start(bf16[128,128]{1,0:T(8,128)(2,1)} %param.11), channel_id=1, source_target_pairs={{0,32},{8,40},{16,48},{24,56},{32,64},{40,72},{48,80},{56,88},{64,... | collective-permute-start | bytes 98312 | tf_op jit(solution)/shard_map/ppermute | solution.py:16
  24.4 9.4 %collective-permute-start.5 = (bf16[128,128]{1,0:T(8,128)(2,1)}, bf16[128,128]{1,0:T(8,128)(2,1)S(1)}, u32[]{:S(2)}, u32[]{:S(2)}) collective-permute-start(bf16[128,128]{1,0:T(8,128)(2,1)} %param.11), channel_id=1, source_target_pairs={{0,24},{8,32},{16,40},{24,48},{32,56},{40,64},{48,72},{56,80},{64,... | collective-permute-start | bytes 98312 | tf_op jit(solution)/shard_map/ppermute | solution.py:16
  26.3 9.4 %collective-permute-start.6 = (bf16[128,128]{1,0:T(8,128)(2,1)}, bf16[128,128]{1,0:T(8,128)(2,1)S(1)}, u32[]{:S(2)}, u32[]{:S(2)}) collective-permute-start(bf16[128,128]{1,0:T(8,128)(2,1)} %param.11), channel_id=1, source_target_pairs={{0,16},{8,24},{16,32},{24,40},{32,48},{40,56},{48,64},{56,72},{64,... | collective-permute-start | bytes 98312 | tf_op jit(solution)/shard_map/ppermute | solution.py:16
  28.5 9.2 %collective-permute-start.7 = (bf16[128,128]{1,0:T(8,128)(2,1)}, bf16[128,128]{1,0:T(8,128)(2,1)S(1)}, u32[]{:S(2)}, u32[]{:S(2)}) collective-permute-start(bf16[128,128]{1,0:T(8,128)(2,1)} %param.11), channel_id=1, source_target_pairs={{0,8},{8,16},{16,24},{24,32},{32,40},{40,48},{48,56},{56,64},{64,7... | collective-permute-start | bytes 98312 | tf_op jit(solution)/shard_map/ppermute | solution.py:16
  30.5 10.6 %collective-permute-start.8 = (bf16[128,128]{1,0:T(8,128)(2,1)}, bf16[128,128]{1,0:T(8,128)(2,1)S(1)}, u32[]{:S(2)}, u32[]{:S(2)}) collective-permute-start(bf16[128,128]{1,0:T(8,128)(2,1)} %param.12), channel_id=1, source_target_pairs={{0,64},{8,72},{16,80},{24,88},{32,96},{40,104},{48,112},{56,120},{... | collective-permute-start | bytes 98312 | tf_op jit(solution)/shard_map/ppermute | solution.py:16
  31.8 12.6 %collective-permute-start.9 = (bf16[128,128]{1,0:T(8,128)(2,1)}, bf16[128,128]{1,0:T(8,128)(2,1)S(1)}, u32[]{:S(2)}, u32[]{:S(2)}) collective-permute-start(bf16[128,128]{1,0:T(8,128)(2,1)} %param.12), channel_id=1, source_target_pairs={{0,56},{8,64},{16,72},{24,80},{32,88},{40,96},{48,104},{56,112},{6... | collective-permute-start | bytes 98312 | tf_op jit(solution)/shard_map/ppermute | solution.py:16
  33.7 13.5 %collective-permute-start.10 = (bf16[128,128]{1,0:T(8,128)(2,1)}, bf16[128,128]{1,0:T(8,128)(2,1)S(1)}, u32[]{:S(2)}, u32[]{:S(2)}) collective-permute-start(bf16[128,128]{1,0:T(8,128)(2,1)} %param.12), channel_id=1, source_target_pairs={{0,48},{8,56},{16,64},{24,72},{32,80},{40,88},{48,96},{56,104},{64... | collective-permute-start | bytes 98312 | tf_op jit(solution)/shard_map/ppermute | solution.py:16
  35.7 13.5 %collective-permute-start.11 = (bf16[128,128]{1,0:T(8,128)(2,1)}, bf16[128,128]{1,0:T(8,128)(2,1)S(1)}, u32[]{:S(2)}, u32[]{:S(2)}) collective-permute-start(bf16[128,128]{1,0:T(8,128)(2,1)} %param.12), channel_id=1, source_target_pairs={{0,40},{8,48},{16,56},{24,64},{32,72},{40,80},{48,88},{56,96},{64,... | collective-permute-start | bytes 98312 | tf_op jit(solution)/shard_map/ppermute | solution.py:16
  37.7 11.6 %collective-permute-start.12 = (bf16[128,128]{1,0:T(8,128)(2,1)}, bf16[128,128]{1,0:T(8,128)(2,1)S(1)}, u32[]{:S(2)}, u32[]{:S(2)}) collective-permute-start(bf16[128,128]{1,0:T(8,128)(2,1)} %param.12), channel_id=1, source_target_pairs={{0,32},{8,40},{16,48},{24,56},{32,64},{40,72},{48,80},{56,88},{64,... | collective-permute-start | bytes 98312 | tf_op jit(solution)/shard_map/ppermute | solution.py:16
  41.0 8.6 %collective-permute-start.13 = (bf16[128,128]{1,0:T(8,128)(2,1)}, bf16[128,128]{1,0:T(8,128)(2,1)S(1)}, u32[]{:S(2)}, u32[]{:S(2)}) collective-permute-start(bf16[128,128]{1,0:T(8,128)(2,1)} %param.12), channel_id=1, source_target_pairs={{0,24},{8,32},{16,40},{24,48},{32,56},{40,64},{48,72},{56,80},{64,... | collective-permute-start | bytes 98312 | tf_op jit(solution)/shard_map/ppermute | solution.py:16
  44.4 8.6 %collective-permute-start.14 = (bf16[128,128]{1,0:T(8,128)(2,1)}, bf16[128,128]{1,0:T(8,128)(2,1)S(1)}, u32[]{:S(2)}, u32[]{:S(2)}) collective-permute-start(bf16[128,128]{1,0:T(8,128)(2,1)} %param.12), channel_id=1, source_target_pairs={{0,16},{8,24},{16,32},{24,40},{32,48},{40,56},{48,64},{56,72},{64,... | collective-permute-start | bytes 98312 | tf_op jit(solution)/shard_map/ppermute | solution.py:16
  47.3 8.1 %collective-permute-start.15 = (bf16[128,128]{1,0:T(8,128)(2,1)}, bf16[128,128]{1,0:T(8,128)(2,1)S(1)}, u32[]{:S(2)}, u32[]{:S(2)}) collective-permute-start(bf16[128,128]{1,0:T(8,128)(2,1)} %param.12), channel_id=1, source_target_pairs={{0,8},{8,16},{16,24},{24,32},{32,40},{40,48},{48,56},{56,64},{64,7... | collective-permute-start | bytes 98312 | tf_op jit(solution)/shard_map/ppermute | solution.py:16
  64.4 126.9 %all-gather.2.cloned.1.call-start = ((), (), s32[]{:S(2)}) async-start(), calls=%async_computation | async-start | bytes 1179648 | tf_op jit(solution)/shard_map/all_gather | solution.py:109
  199.4 22.6 %collective-permute-start.16 = (f32[1,128]{1,0:T(1,128)S(1)}, f32[1,128]{1,0:T(1,128)S(1)}, u32[]{:S(2)}, u32[]{:S(2)}) collective-permute-start(f32[1,128]{1,0:T(1,128)S(1)} %get-tuple-element.257), channel_id=1, source_target_pairs={{8,0},{16,8},{24,16},{32,24},{40,32},{48,40},{56,48},{64,56},{72,6... | collective-permute-start | bytes 1544 | tf_op jit(solution)/shard_map/ppermute | solution.py:16
  204.9 22.2 %collective-permute-start.17 = (f32[1,128]{1,0:T(1,128)S(1)}, f32[1,128]{1,0:T(1,128)S(1)}, u32[]{:S(2)}, u32[]{:S(2)}) collective-permute-start(f32[1,128]{1,0:T(1,128)S(1)} %get-tuple-element.263), channel_id=1, source_target_pairs={{16,0},{24,8},{32,16},{40,24},{48,32},{56,40},{64,48},{72,56},{80,... | collective-permute-start | bytes 1544 | tf_op jit(solution)/shard_map/ppermute | solution.py:16
  207.6 21.5 %collective-permute-start.18 = (f32[1,128]{1,0:T(1,128)S(1)}, f32[1,128]{1,0:T(1,128)S(1)}, u32[]{:S(2)}, u32[]{:S(2)}) collective-permute-start(f32[1,128]{1,0:T(1,128)S(1)} %get-tuple-element.262), channel_id=1, source_target_pairs={{24,0},{32,8},{40,16},{48,24},{56,32},{64,40},{72,48},{80,56},{88,... | collective-permute-start | bytes 1544 | tf_op jit(solution)/shard_map/ppermute | solution.py:16
  211.2 19.4 %collective-permute-start.19 = (f32[1,128]{1,0:T(1,128)S(1)}, f32[1,128]{1,0:T(1,128)S(1)}, u32[]{:S(2)}, u32[]{:S(2)}) collective-permute-start(f32[1,128]{1,0:T(1,128)S(1)} %get-tuple-element.261), channel_id=1, source_target_pairs={{32,0},{40,8},{48,16},{56,24},{64,32},{72,40},{80,48},{88,56},{96,... | collective-permute-start | bytes 1544 | tf_op jit(solution)/shard_map/ppermute | solution.py:16
  215.7 15.0 %collective-permute-start.20 = (f32[1,128]{1,0:T(1,128)S(1)}, f32[1,128]{1,0:T(1,128)S(1)}, u32[]{:S(2)}, u32[]{:S(2)}) collective-permute-start(f32[1,128]{1,0:T(1,128)S(1)} %get-tuple-element.260), channel_id=1, source_target_pairs={{40,0},{48,8},{56,16},{64,24},{72,32},{80,40},{88,48},{96,56},{104... | collective-permute-start | bytes 1544 | tf_op jit(solution)/shard_map/ppermute | solution.py:16
  222.1 8.6 %collective-permute-start.21 = (f32[1,128]{1,0:T(1,128)S(1)}, f32[1,128]{1,0:T(1,128)S(1)}, u32[]{:S(2)}, u32[]{:S(2)}) collective-permute-start(f32[1,128]{1,0:T(1,128)S(1)} %get-tuple-element.259), channel_id=1, source_target_pairs={{48,0},{56,8},{64,16},{72,24},{80,32},{88,40},{96,48},{104,56},{11... | collective-permute-start | bytes 1544 | tf_op jit(solution)/shard_map/ppermute | solution.py:16
  (2 other events, 13.2 us)
Sparse Core Ops, SparseCore 0:
  64.6 93.9 all-reduce.1
  160.7 30.5 all-gather.1
where the time goes:
time: 243 us; the launch traced here: 242 us
  waiting for transfers between devices  138 us (57%)
  starting transfers between devices  66.8 us (27%)
  between operations  15.3 us (6%)
  matrix products  13.3 us (5%)
  local copies, waits for them, and re-layouts  5.22 us (2%)
  other arithmetic  3.65 us (2%)
    psum x1, waiting for transfers between devices, on_device(): lax.psum(jnp.dot(attention, w_out, preferred_element_type=jnp.float32), '...  93.4 us
    ppermute x24, starting transfers between devices, passed_along(): return lax.ppermute(shard, axis, pairs)  66.7 us
    all_gather x1, waiting for transfers between devices, on_device(): lax.all_gather(relevance_out, 'tp', axis=1, tiled=True).astype(jnp.float32)  32.8 us
    ppermute x24, waiting for transfers between devices, passed_along(): return lax.ppermute(shard, axis, pairs)  10.8 us
    dot_general x1, matrix products, on_device(): lax.dot_general(ratio, w_out, (((1,), (1,)), ((), ())), preferred_element...  5.35 us
  transfers between devices with their start and end apart: 26, of which 7 were waited for; matrix products, arithmetic and copies ran while one was open for 2% of the time, Pallas kernels for 0%

commit v1 on v0

--- a/solution.py
+++ b/solution.py
@@ -106,7 +106,9 @@
         .reshape(tokens, local_groups * GROUP * HEAD_DIM)
     )
     totals = lax.psum(jnp.dot(attention, w_out, preferred_element_type=jnp.float32), "tp")
-    upper = lax.all_gather(relevance_out, "tp", axis=1, tiled=True).astype(jnp.float32)
+    upper = jnp.concatenate(
+        lax.all_to_all(jnp.stack([relevance_out] * lax.axis_size("tp")), "tp", 0, 0), axis=1
+    ).astype(jnp.float32)
     ratio = (upper * totals / (totals * totals + 1.0)).astype(jnp.bfloat16)
     carried_back = lax.dot_general(
         ratio, w_out, (((1,), (1,)), ((), ())), preferred_element_type=jnp.float32

time: 243 us -> 215 us (0.88)
  waiting for transfers between devices: 138 us -> 105 us
  starting transfers between devices: 66.8 us -> 72 us
    all_gather x1 -> x0, waiting for transfers between devices: 32.8 us -> none  [on_device(): lax.all_gather(relevance_out, 'tp', axis=1, tiled=True).astype(jnp.float32)]
    all_to_all x0 -> x1, starting transfers between devices: none -> 4.3 us  [on_device(): lax.all_to_all(jnp.stack([relevance_out] * lax.axis_size('tp')), 'tp', 0, 0)]
  transfers between devices with their start and end apart: 26 -> 26, of which waited for: 7 -> 6; matrix products, arithmetic and copies ran while one was open for 2% -> 5% of each run, Pallas kernels for 0% -> 0%
where the time goes in v1:
time: 215 us
  waiting for transfers between devices  105 us (49%)
  starting transfers between devices  72 us (33%)
  between operations  15.4 us (7%)
  matrix products  14.9 us (7%)
  local copies, waits for them, and re-layouts  4.99 us (2%)
  other arithmetic  2.46 us (1%)
    psum x1, waiting for transfers between devices, on_device(): lax.psum(jnp.dot(attention, w_out, preferred_element_type=jnp.float32), '...  93.8 us
    ppermute x24, starting transfers between devices, passed_along(): return lax.ppermute(shard, axis, pairs)  67.7 us
    ppermute x24, waiting for transfers between devices, passed_along(): return lax.ppermute(shard, axis, pairs)  10.8 us
    dot_general x1, matrix products, on_device(): lax.dot_general(ratio, w_out, (((1,), (1,)), ((), ())), preferred_element...  5.05 us
    dot_general x1, matrix products, on_device(): jnp.dot(attention, w_out, preferred_element_type=jnp.float32)  4.32 us
    all_to_all x1, starting transfers between devices, on_device(): lax.all_to_all(jnp.stack([relevance_out] * lax.axis_size('tp')), 'tp', 0, 0)  4.3 us
  transfers between devices with their start and end apart: 26, of which 6 were waited for; matrix products, arithmetic and copies ran while one was open for 5% of the time, Pallas kernels for 0%

profile of v1, /device:TPU:448, one launch (start us, length us, event | category | flops | bytes accessed | tf_op | source)
XLA Modules:
  0.0 214.5 jit_solution(11622115641869812324)
XLA Ops:
  8.6 5.4 %collective-permute-start.1 = (bf16[128,128]{1,0:T(8,128)(2,1)}, bf16[128,128]{1,0:T(8,128)(2,1)S(1)}, u32[]{:S(2)}, u32[]{:S(2)}) collective-permute-start(bf16[128,128]{1,0:T(8,128)(2,1)} %param.11), channel_id=1, source_target_pairs={{0,56},{8,64},{16,72},{24,80},{32,88},{40,96},{48,104},{56,112},{6... | collective-permute-start | bytes 98312 | tf_op jit(solution)/shard_map/ppermute | solution.py:16
  19.8 2.0 stack.2
  21.8 4.3 %all-to-all-start = ((bf16[8,128,512]{2,1,0:T(8,128)(2,1)}), bf16[8,128,512]{2,1,0:T(8,128)(2,1)S(1)}, u32[]{:S(2)}, u32[]{:S(2)}) async-start(bf16[8,128,512]{2,1,0:T(8,128)(2,1)} %stack.2), calls=%async_computation | async-start | bytes 2097152 | tf_op jit(solution)/shard_map/all_to_all | solution.py:110
  27.8 1.9 collective-permute-start.5
  29.8 2.1 collective-permute-start.6
  31.9 1.9 collective-permute-start.7
  35.3 1.9 collective-permute-start.9
  43.9 3.3 %collective-permute-start.13 = (bf16[128,128]{1,0:T(8,128)(2,1)S(1)}, bf16[128,128]{1,0:T(8,128)(2,1)S(1)}, u32[]{:S(2)}, u32[]{:S(2)}) collective-permute-start(bf16[128,128]{1,0:T(8,128)(2,1)S(1)} %copy-done.9), channel_id=1, source_target_pairs={{0,24},{8,32},{16,40},{24,48},{32,56},{40,64},{48,72},{56,80},{64,... | collective-permute-start | bytes 98312 | tf_op jit(solution)/shard_map/ppermute | solution.py:16
  47.3 2.8 %collective-permute-start.14 = (bf16[128,128]{1,0:T(8,128)(2,1)S(1)}, bf16[128,128]{1,0:T(8,128)(2,1)S(1)}, u32[]{:S(2)}, u32[]{:S(2)}) collective-permute-start(bf16[128,128]{1,0:T(8,128)(2,1)S(1)} %copy-done.9), channel_id=1, source_target_pairs={{0,16},{8,24},{16,32},{24,40},{32,48},{40,56},{48,64},{56,72},{64,... | collective-permute-start | bytes 98312 | tf_op jit(solution)/shard_map/ppermute | solution.py:16
  52.5 3.4 %collective-permute-done.14 = bf16[128,128]{1,0:T(8,128)(2,1)S(1)} collective-permute-done((bf16[128,128]{1,0:T(8,128)(2,1)S(1)}, bf16[128,128]{1,0:T(8,128)(2,1)S(1)}, u32[]{:S(2)}, u32[]{:S(2)}) %collective-permute-start.14) | collective-permute-done | bytes 32800 | tf_op jit(solution)/shard_map/ppermute | solution.py:16
  55.9 2.2 %collective-permute-done.15 = bf16[128,128]{1,0:T(8,128)(2,1)S(1)} collective-permute-done((bf16[128,128]{1,0:T(8,128)(2,1)S(1)}, bf16[128,128]{1,0:T(8,128)(2,1)S(1)}, u32[]{:S(2)}, u32[]{:S(2)}) %collective-permute-start.15) | collective-permute-done | bytes 32800 | tf_op jit(solution)/shard_map/ppermute | solution.py:16
  58.2 3.6 %while.26 = (s32[]{:T(128)}, f32[1,512]{1,0:T(1,128)S(1)}, f32[1,512]{1,0:T(1,128)S(1)}, f32[1,512,128]{2,1,0:T(8,128)S(1)}, s32[]{:T(128)}, /*index=5*/s32[1536...) while((s32[]{:T(128)}, f32[1,512]{1,0:T(1,128)S(1)}, ...), condition=%wide.region_4.5_spmd.clone, body=%wide.region_1.4_spmd.clone.sunk | while | flops 139069440 | bytes 4139747 | solution.py:101
  62.7 4.3 %fusion.48 = f32[128,4096]{1,0:T(8,128)} fusion(bf16[128,512]{1,0:T(8,128)(2,1)S(1)} %reshape_transpose_reshape.10, bf16[512,4096]{1,0:T(8,128)(2,1)} %param.13), kind=kOutput, calls=%fused_computation.95 | convolution fusion | flops 536870912 | bytes 6422528 | tf_op jit(solution)/shard_map/dot_general | solution.py:108
  67.6 93.8 %all-reduce.2.cloned.1.call-done = f32[128,4096]{1,0:T(8,128)} async-done(((f32[128,4096]{1,0:T(8,128)}), f32[128,4096]{1,0:T(8,128)}) %all-reduce.2.cloned.1.call-update) | async-done | bytes 2097168 | tf_op jit(solution)/shard_map/psum | solution.py:108
  161.4 5.0 %fusion.43 = (bf16[128,512]{1,0:T(8,128)(2,1)S(1)}, bf16[128,512]{1,0:T(8,128)(2,1)}) fusion(bf16[128,512]{1,0:T(8,128)(2,1)S(1)} %copy-done.1, bf16[512,4096]{1,0:T(8,128)(2,1)} %param.13, f32[128,4096]{1,0:T(8,128)} %all-reduce.2.cloned.1.call-done, f32[128,4096]{1,0:T(8,128)S(1)} %bitcast.98), kind=kOutput, calls=%fused_computation.57 | convolution fusion | flops 540016640 | bytes 8781824 | tf_op jit(solution)/shard_map/dot_general | solution.py:113
  166.6 4.4 %while.27 = (s32[]{:T(128)}, f32[1,1536]{1,0:T(1,128)S(1)}, s32[]{:T(128)}, s32[1536]{0:T(1024)S(1)}, s32[]{:T(128)}, /*index=5*/bf16[1536,1,128]{2,0,1:T(8,128)...) while((s32[]{:T(128)}, f32[1,1536]{1,0:T(1,128)S(1)}, ...), condition=%wide.region_8.9_spmd.clone, body=%wide.region_6.8_spmd.clone.sunk | while | flops 136578048 | bytes 2661103 | solution.py:134
  171.0 5.5 %collective-permute-start.16 = (f32[1,128]{1,0:T(1,128)S(1)}, f32[1,128]{1,0:T(1,128)S(1)}, u32[]{:S(2)}, u32[]{:S(2)}) collective-permute-start(f32[1,128]{1,0:T(1,128)S(1)} %get-tuple-element.257), channel_id=1, source_target_pairs={{8,0},{16,8},{24,16},{32,24},{40,32},{48,40},{56,48},{64,56},{72,6... | collective-permute-start | bytes 1544 | tf_op jit(solution)/shard_map/ppermute | solution.py:16
  176.5 2.7 %collective-permute-start.17 = (f32[1,128]{1,0:T(1,128)S(1)}, f32[1,128]{1,0:T(1,128)S(1)}, u32[]{:S(2)}, u32[]{:S(2)}) collective-permute-start(f32[1,128]{1,0:T(1,128)S(1)} %get-tuple-element.263), channel_id=1, source_target_pairs={{16,0},{24,8},{32,16},{40,24},{48,32},{56,40},{64,48},{72,56},{80,... | collective-permute-start | bytes 1544 | tf_op jit(solution)/shard_map/ppermute | solution.py:16
  179.2 3.6 %collective-permute-start.18 = (f32[1,128]{1,0:T(1,128)S(1)}, f32[1,128]{1,0:T(1,128)S(1)}, u32[]{:S(2)}, u32[]{:S(2)}) collective-permute-start(f32[1,128]{1,0:T(1,128)S(1)} %get-tuple-element.262), channel_id=1, source_target_pairs={{24,0},{32,8},{40,16},{48,24},{56,32},{64,40},{72,48},{80,56},{88,... | collective-permute-start | bytes 1544 | tf_op jit(solution)/shard_map/ppermute | solution.py:16
  182.8 4.5 %collective-permute-start.19 = (f32[1,128]{1,0:T(1,128)S(1)}, f32[1,128]{1,0:T(1,128)S(1)}, u32[]{:S(2)}, u32[]{:S(2)}) collective-permute-start(f32[1,128]{1,0:T(1,128)S(1)} %get-tuple-element.261), channel_id=1, source_target_pairs={{32,0},{40,8},{48,16},{56,24},{64,32},{72,40},{80,48},{88,56},{96,... | collective-permute-start | bytes 1544 | tf_op jit(solution)/shard_map/ppermute | solution.py:16
  187.3 7.2 %collective-permute-start.20 = (f32[1,128]{1,0:T(1,128)S(1)}, f32[1,128]{1,0:T(1,128)S(1)}, u32[]{:S(2)}, u32[]{:S(2)}) collective-permute-start(f32[1,128]{1,0:T(1,128)S(1)} %get-tuple-element.260), channel_id=1, source_target_pairs={{40,0},{48,8},{56,16},{64,24},{72,32},{80,40},{88,48},{96,56},{104... | collective-permute-start | bytes 1544 | tf_op jit(solution)/shard_map/ppermute | solution.py:16
  194.6 5.0 %collective-permute-start.21 = (f32[1,128]{1,0:T(1,128)S(1)}, f32[1,128]{1,0:T(1,128)S(1)}, u32[]{:S(2)}, u32[]{:S(2)}) collective-permute-start(f32[1,128]{1,0:T(1,128)S(1)} %get-tuple-element.259), channel_id=1, source_target_pairs={{48,0},{56,8},{64,16},{72,24},{80,32},{88,40},{96,48},{104,56},{11... | collective-permute-start | bytes 1544 | tf_op jit(solution)/shard_map/ppermute | solution.py:16
  199.6 1.9 collective-permute-start.22
  203.2 4.0 %collective-permute-done.22 = f32[1,128]{1,0:T(1,128)S(1)} collective-permute-done((f32[1,128]{1,0:T(1,128)S(1)}, f32[1,128]{1,0:T(1,128)S(1)}, u32[]{:S(2)}, u32[]{:S(2)}) %collective-permute-start.22) | collective-permute-done | bytes 544 | tf_op jit(solution)/shard_map/ppermute | solution.py:16
  (134 shorter events, 30.0 us)
Async XLA Ops:
  7.2 20.6 %collective-permute-start = (bf16[128,128]{1,0:T(8,128)(2,1)}, bf16[128,128]{1,0:T(8,128)(2,1)S(1)}, u32[]{:S(2)}, u32[]{:S(2)}) collective-permute-start(bf16[128,128]{1,0:T(8,128)(2,1)} %param.11), channel_id=1, source_target_pairs={{0,64},{8,72},{16,80},{24,88},{32,96},{40,104},{48,112},{56,120},{... | collective-permute-start | bytes 98312 | tf_op jit(solution)/shard_map/ppermute | solution.py:16
  8.6 21.2 %collective-permute-start.1 = (bf16[128,128]{1,0:T(8,128)(2,1)}, bf16[128,128]{1,0:T(8,128)(2,1)S(1)}, u32[]{:S(2)}, u32[]{:S(2)}) collective-permute-start(bf16[128,128]{1,0:T(8,128)(2,1)} %param.11), channel_id=1, source_target_pairs={{0,56},{8,64},{16,72},{24,80},{32,88},{40,96},{48,104},{56,112},{6... | collective-permute-start | bytes 98312 | tf_op jit(solution)/shard_map/ppermute | solution.py:16
  14.0 17.9 %collective-permute-start.2 = (bf16[128,128]{1,0:T(8,128)(2,1)}, bf16[128,128]{1,0:T(8,128)(2,1)S(1)}, u32[]{:S(2)}, u32[]{:S(2)}) collective-permute-start(bf16[128,128]{1,0:T(8,128)(2,1)} %param.11), channel_id=1, source_target_pairs={{0,48},{8,56},{16,64},{24,72},{32,80},{40,88},{48,96},{56,104},{64... | collective-permute-start | bytes 98312 | tf_op jit(solution)/shard_map/ppermute | solution.py:16
  15.9 18.0 %collective-permute-start.3 = (bf16[128,128]{1,0:T(8,128)(2,1)}, bf16[128,128]{1,0:T(8,128)(2,1)S(1)}, u32[]{:S(2)}, u32[]{:S(2)}) collective-permute-start(bf16[128,128]{1,0:T(8,128)(2,1)} %param.11), channel_id=1, source_target_pairs={{0,40},{8,48},{16,56},{24,64},{32,72},{40,80},{48,88},{56,96},{64,... | collective-permute-start | bytes 98312 | tf_op jit(solution)/shard_map/ppermute | solution.py:16
  17.9 17.4 %collective-permute-start.4 = (bf16[128,128]{1,0:T(8,128)(2,1)}, bf16[128,128]{1,0:T(8,128)(2,1)S(1)}, u32[]{:S(2)}, u32[]{:S(2)}) collective-permute-start(bf16[128,128]{1,0:T(8,128)(2,1)} %param.11), channel_id=1, source_target_pairs={{0,32},{8,40},{16,48},{24,56},{32,64},{40,72},{48,80},{56,88},{64,... | collective-permute-start | bytes 98312 | tf_op jit(solution)/shard_map/ppermute | solution.py:16
  21.8 45.3 %all-to-all-start = ((bf16[8,128,512]{2,1,0:T(8,128)(2,1)}), bf16[8,128,512]{2,1,0:T(8,128)(2,1)S(1)}, u32[]{:S(2)}, u32[]{:S(2)}) async-start(bf16[8,128,512]{2,1,0:T(8,128)(2,1)} %stack.2), calls=%async_computation | async-start | bytes 2097152 | tf_op jit(solution)/shard_map/all_to_all | solution.py:110
  26.1 135.3 %all-reduce.2.cloned.1.call-start = ((), (), s32[]{:S(2)}) async-start(), calls=%async_computation.1 | async-start | bytes 4194304 | tf_op jit(solution)/shard_map/psum | solution.py:108
  27.8 9.4 %collective-permute-start.5 = (bf16[128,128]{1,0:T(8,128)(2,1)S(1)}, bf16[128,128]{1,0:T(8,128)(2,1)S(1)}, u32[]{:S(2)}, u32[]{:S(2)}) collective-permute-start(bf16[128,128]{1,0:T(8,128)(2,1)S(1)} %copy-done.8), channel_id=1, source_target_pairs={{0,24},{8,32},{16,40},{24,48},{32,56},{40,64},{48,72},{56,80},{64,... | collective-permute-start | bytes 98312 | tf_op jit(solution)/shard_map/ppermute | solution.py:16
  29.8 9.4 %collective-permute-start.6 = (bf16[128,128]{1,0:T(8,128)(2,1)S(1)}, bf16[128,128]{1,0:T(8,128)(2,1)S(1)}, u32[]{:S(2)}, u32[]{:S(2)}) collective-permute-start(bf16[128,128]{1,0:T(8,128)(2,1)S(1)} %copy-done.8), channel_id=1, source_target_pairs={{0,16},{8,24},{16,32},{24,40},{32,48},{40,56},{48,64},{56,72},{64,... | collective-permute-start | bytes 98312 | tf_op jit(solution)/shard_map/ppermute | solution.py:16
  31.9 9.2 %collective-permute-start.7 = (bf16[128,128]{1,0:T(8,128)(2,1)S(1)}, bf16[128,128]{1,0:T(8,128)(2,1)S(1)}, u32[]{:S(2)}, u32[]{:S(2)}) collective-permute-start(bf16[128,128]{1,0:T(8,128)(2,1)S(1)} %copy-done.8), channel_id=1, source_target_pairs={{0,8},{8,16},{16,24},{24,32},{32,40},{40,48},{48,56},{56,64},{64,7... | collective-permute-start | bytes 98312 | tf_op jit(solution)/shard_map/ppermute | solution.py:16
  33.9 10.0 %collective-permute-start.8 = (bf16[128,128]{1,0:T(8,128)(2,1)S(1)}, bf16[128,128]{1,0:T(8,128)(2,1)S(1)}, u32[]{:S(2)}, u32[]{:S(2)}) collective-permute-start(bf16[128,128]{1,0:T(8,128)(2,1)S(1)} %copy-done.9), channel_id=1, source_target_pairs={{0,64},{8,72},{16,80},{24,88},{32,96},{40,104},{48,112},{56,120},{... | collective-permute-start | bytes 98312 | tf_op jit(solution)/shard_map/ppermute | solution.py:16
  35.3 12.0 %collective-permute-start.9 = (bf16[128,128]{1,0:T(8,128)(2,1)S(1)}, bf16[128,128]{1,0:T(8,128)(2,1)S(1)}, u32[]{:S(2)}, u32[]{:S(2)}) collective-permute-start(bf16[128,128]{1,0:T(8,128)(2,1)S(1)} %copy-done.9), channel_id=1, source_target_pairs={{0,56},{8,64},{16,72},{24,80},{32,88},{40,96},{48,104},{56,112},{6... | collective-permute-start | bytes 98312 | tf_op jit(solution)/shard_map/ppermute | solution.py:16
  37.2 12.9 %collective-permute-start.10 = (bf16[128,128]{1,0:T(8,128)(2,1)S(1)}, bf16[128,128]{1,0:T(8,128)(2,1)S(1)}, u32[]{:S(2)}, u32[]{:S(2)}) collective-permute-start(bf16[128,128]{1,0:T(8,128)(2,1)S(1)} %copy-done.9), channel_id=1, source_target_pairs={{0,48},{8,56},{16,64},{24,72},{32,80},{40,88},{48,96},{56,104},{64... | collective-permute-start | bytes 98312 | tf_op jit(solution)/shard_map/ppermute | solution.py:16
  39.2 12.9 %collective-permute-start.11 = (bf16[128,128]{1,0:T(8,128)(2,1)S(1)}, bf16[128,128]{1,0:T(8,128)(2,1)S(1)}, u32[]{:S(2)}, u32[]{:S(2)}) collective-permute-start(bf16[128,128]{1,0:T(8,128)(2,1)S(1)} %copy-done.9), channel_id=1, source_target_pairs={{0,40},{8,48},{16,56},{24,64},{32,72},{40,80},{48,88},{56,96},{64,... | collective-permute-start | bytes 98312 | tf_op jit(solution)/shard_map/ppermute | solution.py:16
  41.1 11.0 %collective-permute-start.12 = (bf16[128,128]{1,0:T(8,128)(2,1)S(1)}, bf16[128,128]{1,0:T(8,128)(2,1)S(1)}, u32[]{:S(2)}, u32[]{:S(2)}) collective-permute-start(bf16[128,128]{1,0:T(8,128)(2,1)S(1)} %copy-done.9), channel_id=1, source_target_pairs={{0,32},{8,40},{16,48},{24,56},{32,64},{40,72},{48,80},{56,88},{64,... | collective-permute-start | bytes 98312 | tf_op jit(solution)/shard_map/ppermute | solution.py:16
  43.9 8.6 %collective-permute-start.13 = (bf16[128,128]{1,0:T(8,128)(2,1)S(1)}, bf16[128,128]{1,0:T(8,128)(2,1)S(1)}, u32[]{:S(2)}, u32[]{:S(2)}) collective-permute-start(bf16[128,128]{1,0:T(8,128)(2,1)S(1)} %copy-done.9), channel_id=1, source_target_pairs={{0,24},{8,32},{16,40},{24,48},{32,56},{40,64},{48,72},{56,80},{64,... | collective-permute-start | bytes 98312 | tf_op jit(solution)/shard_map/ppermute | solution.py:16
  47.3 8.6 %collective-permute-start.14 = (bf16[128,128]{1,0:T(8,128)(2,1)S(1)}, bf16[128,128]{1,0:T(8,128)(2,1)S(1)}, u32[]{:S(2)}, u32[]{:S(2)}) collective-permute-start(bf16[128,128]{1,0:T(8,128)(2,1)S(1)} %copy-done.9), channel_id=1, source_target_pairs={{0,16},{8,24},{16,32},{24,40},{32,48},{40,56},{48,64},{56,72},{64,... | collective-permute-start | bytes 98312 | tf_op jit(solution)/shard_map/ppermute | solution.py:16
  50.2 7.9 %collective-permute-start.15 = (bf16[128,128]{1,0:T(8,128)(2,1)S(1)}, bf16[128,128]{1,0:T(8,128)(2,1)S(1)}, u32[]{:S(2)}, u32[]{:S(2)}) collective-permute-start(bf16[128,128]{1,0:T(8,128)(2,1)S(1)} %copy-done.9), channel_id=1, source_target_pairs={{0,8},{8,16},{16,24},{24,32},{32,40},{40,48},{48,56},{56,64},{64,7... | collective-permute-start | bytes 98312 | tf_op jit(solution)/shard_map/ppermute | solution.py:16
  171.0 23.5 %collective-permute-start.16 = (f32[1,128]{1,0:T(1,128)S(1)}, f32[1,128]{1,0:T(1,128)S(1)}, u32[]{:S(2)}, u32[]{:S(2)}) collective-permute-start(f32[1,128]{1,0:T(1,128)S(1)} %get-tuple-element.257), channel_id=1, source_target_pairs={{8,0},{16,8},{24,16},{32,24},{40,32},{48,40},{56,48},{64,56},{72,6... | collective-permute-start | bytes 1544 | tf_op jit(solution)/shard_map/ppermute | solution.py:16
  176.5 23.1 %collective-permute-start.17 = (f32[1,128]{1,0:T(1,128)S(1)}, f32[1,128]{1,0:T(1,128)S(1)}, u32[]{:S(2)}, u32[]{:S(2)}) collective-permute-start(f32[1,128]{1,0:T(1,128)S(1)} %get-tuple-element.263), channel_id=1, source_target_pairs={{16,0},{24,8},{32,16},{40,24},{48,32},{56,40},{64,48},{72,56},{80,... | collective-permute-start | bytes 1544 | tf_op jit(solution)/shard_map/ppermute | solution.py:16
  179.2 22.3 %collective-permute-start.18 = (f32[1,128]{1,0:T(1,128)S(1)}, f32[1,128]{1,0:T(1,128)S(1)}, u32[]{:S(2)}, u32[]{:S(2)}) collective-permute-start(f32[1,128]{1,0:T(1,128)S(1)} %get-tuple-element.262), channel_id=1, source_target_pairs={{24,0},{32,8},{40,16},{48,24},{56,32},{64,40},{72,48},{80,56},{88,... | collective-permute-start | bytes 1544 | tf_op jit(solution)/shard_map/ppermute | solution.py:16
  182.8 20.4 %collective-permute-start.19 = (f32[1,128]{1,0:T(1,128)S(1)}, f32[1,128]{1,0:T(1,128)S(1)}, u32[]{:S(2)}, u32[]{:S(2)}) collective-permute-start(f32[1,128]{1,0:T(1,128)S(1)} %get-tuple-element.261), channel_id=1, source_target_pairs={{32,0},{40,8},{48,16},{56,24},{64,32},{72,40},{80,48},{88,56},{96,... | collective-permute-start | bytes 1544 | tf_op jit(solution)/shard_map/ppermute | solution.py:16
  187.3 15.9 %collective-permute-start.20 = (f32[1,128]{1,0:T(1,128)S(1)}, f32[1,128]{1,0:T(1,128)S(1)}, u32[]{:S(2)}, u32[]{:S(2)}) collective-permute-start(f32[1,128]{1,0:T(1,128)S(1)} %get-tuple-element.260), channel_id=1, source_target_pairs={{40,0},{48,8},{56,16},{64,24},{72,32},{80,40},{88,48},{96,56},{104... | collective-permute-start | bytes 1544 | tf_op jit(solution)/shard_map/ppermute | solution.py:16
  194.6 8.6 %collective-permute-start.21 = (f32[1,128]{1,0:T(1,128)S(1)}, f32[1,128]{1,0:T(1,128)S(1)}, u32[]{:S(2)}, u32[]{:S(2)}) collective-permute-start(f32[1,128]{1,0:T(1,128)S(1)} %get-tuple-element.259), channel_id=1, source_target_pairs={{48,0},{56,8},{64,16},{72,24},{80,32},{88,40},{96,48},{104,56},{11... | collective-permute-start | bytes 1544 | tf_op jit(solution)/shard_map/ppermute | solution.py:16
  (13 other events, 219.9 us)
Sparse Core Ops, SparseCore 0:
  67.2 94.1 all-reduce.1
